TPU v7x, 32 devices: a whole 2x2x4 slice. The times are simulated.
32 devices in a mesh: grp: 2 (over y), lvl: 4 (over x, core), col: 4 (over z).
Axes of the slice: x: 2, y: 2, z: 4, core: 2. Of those that a mesh axis runs over, the one named last changes fastest.
Arguments:
- inverse_diag: float32 [64, 256, 256], P(('grp', 'lvl')), parts along dimension 0, may hold values from 0 to 2, as said below
- down_block: float32 [64, 256, 256], P(('grp', 'lvl')), parts along dimension 0, may hold values from 0 to 2, as said below
- up_block: float32 [64, 256, 256], P(('grp', 'lvl')), parts along dimension 0, may hold values from 0 to 1, as said below
- reward: float32 [64, 64, 256], P(('grp', 'lvl'), 'col'), parts along dimension 0, may hold values from -6 to 6
Outputs:
- values: float32 [64, 64, 256], P(('grp', 'lvl'), 'col'), parts along dimension 0
There are 2 independent parts, one for each index of `grp`. A program takes and returns all parts, laid end to end along the dimension named above; each array names one. Nothing has to cross between parts.
Inputs may be any that keep to these rules, and one draw needn't show every extreme that they name: `inverse_diag`: Nonnegative. `down_block`: Nonnegative. `up_block`: Nonnegative.
All inputs are finite; a program needn't handle non-finite values.
Results may differ from a plain program's by a relative error of at most 0.00011.
Values sent between devices are 32-bit elements; how exact they have to be, the bound alone decides.
A program may use at most 64 MiB of HBM per device.

v0:
```python
import jax
import jax.numpy as jnp
from jax import lax
from jax.sharding import PartitionSpec as P

SWEEPS = 8


PRECISE = lax.Precision.HIGHEST


def from_behind(value, axis, steps):
    count = lax.axis_size(axis)
    first, last = (max(0, -steps), min(count, count - steps))
    return lax.ppermute(value, axis, [(source, source + steps) for source in range(first, last)])


def entering_2(part, axis, combine, identity):
    place = lax.axis_index(axis)
    gathered = jax.tree.map(lambda a: lax.all_gather(a, axis), part)
    state = jax.tree.map(lambda a, e: jnp.zeros_like(a) + jnp.asarray(e, a.dtype), part, identity)

    def one(step, state):
        return combine(
            state, jax.tree.map(lambda a: lax.dynamic_index_in_dim(a, step, 0, False), gathered)
        )

    return lax.fori_loop(0, place, one, state)


def apply_right(vector, matrix):
    return jnp.einsum("km,pm->kp", vector, matrix, precision=PRECISE)


def local_sweep(entering, inverse_diag, down_block, base_terms):

    def level_step(carried, inputs):
        inv_here, down_here, base_here = inputs
        updated = apply_right(base_here + apply_right(carried, down_here), inv_here)
        return (updated, updated)

    return lax.scan(level_step, entering, (inverse_diag, down_block, base_terms))


def transfer_full(inverse_diag, down_block):
    identity_mat = jnp.eye(inverse_diag.shape[1], dtype=jnp.float32)

    def compose(product, inputs):
        inv_here, down_here = inputs
        return (
            jnp.matmul(
                inv_here, jnp.matmul(down_here, product, precision=PRECISE), precision=PRECISE
            ),
            None,
        )

    result, _ = lax.scan(compose, identity_mat, (inverse_diag, down_block))
    return result


def local(inverse_diag, down_block, up_block, reward):
    phases = reward.shape[2]
    identity_mat = jnp.eye(phases, dtype=jnp.float32)
    transfer = transfer_full(inverse_diag, down_block)
    estimate = jnp.zeros_like(reward)
    for repeat in range(SWEEPS):
        rim_values = from_behind(estimate[0], "lvl", -1)
        beyond = jnp.concatenate([estimate[1:], rim_values[None]], axis=0)
        base_terms = reward + jnp.einsum("lkm,lpm->lkp", beyond, up_block, precision=PRECISE)
        outgoing, _ = local_sweep(jnp.zeros_like(reward[0]), inverse_diag, down_block, base_terms)

        def compose_maps(earlier, later):
            joined = jnp.matmul(later[0], earlier[0], precision=PRECISE)
            return (joined, apply_right(earlier[1], later[0]) + later[1])

        prefix = entering_2(
            (transfer, outgoing), "lvl", compose_maps, (identity_mat, jnp.zeros_like(outgoing))
        )
        entering = prefix[1]
        _, estimate = local_sweep(entering, inverse_diag, down_block, base_terms)
    return estimate


def solution(mesh):
    placed = (
        P(("grp", "lvl"), None, None),
        P(("grp", "lvl"), None, None),
        P(("grp", "lvl"), None, None),
        P(("grp", "lvl"), "col", None),
    )
    return jax.shard_map(
        local, mesh=mesh, in_specs=placed, out_specs=P(("grp", "lvl"), "col", None), check_vma=False
    )
```

profile of v0, /device:TPU:11, one launch (start us, length us, event | category | flops | bytes accessed | tf_op | source)
XLA Modules:
  0.0 493.2 jit_solution(10380933580429825770)
XLA Ops:
  6.5 2.7 collective-permute-start
  9.3 21.6 %while.282 = (s32[]{:T(128)}, f32[256,256]{1,0:T(8,128)S(1)}, f32[8,256,256]{2,1,0:T(8,128)}, f32[8,256,256]{2,1,0:T(8,128)}, s32[]{:T(128)}) while((s32[]{:T(128)}, f32[256,256]{1,0:T(8,128)S(1)}, f32[8,256,256]{2,1,0:T(8,128)}, f32[8,256,256]{2,1,0:T(8,128)}, s32[]{:T(128)}) %tuple.378), condition=%wide.region_1.2_spmd, body=%wide.region_0.1_spmd.sunk | while | flops 402653184 | bytes 1573949 | solution.py:57
  33.5 20.4 %while.283 = (s32[]{:T(128)}, f32[16,256]{1,0:T(8,128)S(1)}, f32[8,16,256]{2,1,0:T(8,128)S(1)}, f32[8,256,256]{2,1,0:T(8,128)}, f32[8,256,256]{2,1,0:T(8,128)}, /*index=5*/s32[]{:T(128)}) while((s32[]{:T(128)}, f32[16,256]{1,0:T(8,128)S(1)}, f32[8,16,256]{2,1,0:T(8,128)S(1)}, f32[8,256,256]{2,1,0:T(8,128)}, f32[8,256,256]{2,1,0:T(8,128)}, ...), condition=%wide.region_3.4_spmd, body=%wide.region_2.3_spmd.sunk | while | flops 25169920 | bytes 607813 | solution.py:42
  53.9 5.1 %all-gather.1 = f32[64,256]{1,0:T(8,128)S(1)} all-gather(f32[16,256]{1,0:T(8,128)S(1)} %get-tuple-element.852), channel_id=3, replica_groups=mesh['grp'=2,'lvl'=4,'col'=4] {'lvl'}, dimensions={0}, use_global_device_ids=true | all-gather | bytes 81920 | tf_op jit(solution)/shard_map/all_gather | solution.py:20
  59.0 3.9 while.284
  63.0 20.4 %while.285 = (s32[]{:T(128)}, f32[16,256]{1,0:T(8,128)S(1)}, f32[8,16,256]{2,1,0:T(8,128)S(1)}, f32[8,16,256]{2,1,0:T(8,128)S(1)}, f32[8,256,256]{2,1,0:T(8,128)}, /*index=5*/f32[8,256,256]{2,1,0:T(8,128)}, s32[]{:T(128)}) while((s32[]{:T(128)}, f32[16,256]{1,0:T(8,128)S(1)}, f32[8,16,256]{2,1,0:T(8,128)S(1)}, f32[8,16,256]{2,1,0:T(8,128)S(1)}, ...), condition=%wide.region_7.8_spmd, body=%wide.region_6.7_spmd.sunk | while | flops 25169920 | bytes 624717 | solution.py:42
  87.4 20.4 %while.286 = (s32[]{:T(128)}, f32[16,256]{1,0:T(8,128)S(1)}, f32[8,16,256]{2,1,0:T(8,128)S(1)}, f32[8,256,256]{2,1,0:T(8,128)}, f32[8,256,256]{2,1,0:T(8,128)}, /*index=5*/s32[]{:T(128)}) while((s32[]{:T(128)}, f32[16,256]{1,0:T(8,128)S(1)}, f32[8,16,256]{2,1,0:T(8,128)S(1)}, f32[8,256,256]{2,1,0:T(8,128)}, f32[8,256,256]{2,1,0:T(8,128)}, ...), condition=%wide.region_9.10_spmd, body=%wide.region_8.9_spmd.sunk | while | flops 25169920 | bytes 607813 | solution.py:42
  107.8 5.5 %all-gather.2 = f32[64,256]{1,0:T(8,128)S(1)} all-gather(f32[16,256]{1,0:T(8,128)S(1)} %get-tuple-element.855), channel_id=4, replica_groups=mesh['grp'=2,'lvl'=4,'col'=4] {'lvl'}, dimensions={0}, use_global_device_ids=true | all-gather | bytes 81920 | tf_op jit(solution)/shard_map/all_gather | solution.py:20
  115.0 25.3 %while.288 = (s32[]{:T(128)}, f32[16,256]{1,0:T(8,128)S(1)}, f32[8,16,256]{2,1,0:T(8,128)}, f32[8,16,256]{2,1,0:T(8,128)S(1)}, f32[8,256,256]{2,1,0:T(8,128)}, /*index=5*/f32[8,256,256]{2,1,0:T(8,128)}, s32[]{:T(128)}) while((s32[]{:T(128)}, f32[16,256]{1,0:T(8,128)S(1)}, f32[8,16,256]{2,1,0:T(8,128)}, f32[8,16,256]{2,1,0:T(8,128)S(1)}, ...), condition=%wide.region_13.14_spmd, body=%wide.region_12.13_spmd.sunk | while | flops 25169920 | bytes 624717 | solution.py:42
  116.3 1.9 bitcast_dynamic-update-slice_fusion.17
  119.4 1.9 bitcast_dynamic-update-slice_fusion.17
  122.6 1.9 bitcast_dynamic-update-slice_fusion.17
  125.8 1.9 bitcast_dynamic-update-slice_fusion.17
  128.9 1.9 bitcast_dynamic-update-slice_fusion.17
  145.5 20.4 %while.289 = (s32[]{:T(128)}, f32[16,256]{1,0:T(8,128)S(1)}, f32[8,16,256]{2,1,0:T(8,128)S(1)}, f32[8,256,256]{2,1,0:T(8,128)}, f32[8,256,256]{2,1,0:T(8,128)}, /*index=5*/s32[]{:T(128)}) while((s32[]{:T(128)}, f32[16,256]{1,0:T(8,128)S(1)}, f32[8,16,256]{2,1,0:T(8,128)S(1)}, f32[8,256,256]{2,1,0:T(8,128)}, f32[8,256,256]{2,1,0:T(8,128)}, ...), condition=%wide.region_15.16_spmd, body=%wide.region_14.15_spmd.sunk | while | flops 25169920 | bytes 607813 | solution.py:42
  165.9 5.7 %all-gather.3 = f32[64,256]{1,0:T(8,128)S(1)} all-gather(f32[16,256]{1,0:T(8,128)S(1)} %get-tuple-element.858), channel_id=5, replica_groups=mesh['grp'=2,'lvl'=4,'col'=4] {'lvl'}, dimensions={0}, use_global_device_ids=true | all-gather | bytes 81920 | tf_op jit(solution)/shard_map/all_gather | solution.py:20
  173.3 25.3 %while.291 = (s32[]{:T(128)}, f32[16,256]{1,0:T(8,128)S(1)}, f32[8,16,256]{2,1,0:T(8,128)}, f32[8,16,256]{2,1,0:T(8,128)S(1)}, f32[8,256,256]{2,1,0:T(8,128)}, /*index=5*/f32[8,256,256]{2,1,0:T(8,128)}, s32[]{:T(128)}) while((s32[]{:T(128)}, f32[16,256]{1,0:T(8,128)S(1)}, f32[8,16,256]{2,1,0:T(8,128)}, f32[8,16,256]{2,1,0:T(8,128)S(1)}, ...), condition=%wide.region_19.20_spmd, body=%wide.region_18.19_spmd.sunk | while | flops 25169920 | bytes 624717 | solution.py:42
  203.8 20.4 %while.292 = (s32[]{:T(128)}, f32[16,256]{1,0:T(8,128)S(1)}, f32[8,16,256]{2,1,0:T(8,128)S(1)}, f32[8,256,256]{2,1,0:T(8,128)}, f32[8,256,256]{2,1,0:T(8,128)}, /*index=5*/s32[]{:T(128)}) while((s32[]{:T(128)}, f32[16,256]{1,0:T(8,128)S(1)}, f32[8,16,256]{2,1,0:T(8,128)S(1)}, f32[8,256,256]{2,1,0:T(8,128)}, f32[8,256,256]{2,1,0:T(8,128)}, ...), condition=%wide.region_21.22_spmd, body=%wide.region_20.21_spmd.sunk | while | flops 25169920 | bytes 607813 | solution.py:42
  224.3 5.8 %all-gather.4 = f32[64,256]{1,0:T(8,128)S(1)} all-gather(f32[16,256]{1,0:T(8,128)S(1)} %get-tuple-element.861), channel_id=6, replica_groups=mesh['grp'=2,'lvl'=4,'col'=4] {'lvl'}, dimensions={0}, use_global_device_ids=true | all-gather | bytes 81920 | tf_op jit(solution)/shard_map/all_gather | solution.py:20
  232.0 25.3 %while.294 = (s32[]{:T(128)}, f32[16,256]{1,0:T(8,128)S(1)}, f32[8,16,256]{2,1,0:T(8,128)}, f32[8,16,256]{2,1,0:T(8,128)S(1)}, f32[8,256,256]{2,1,0:T(8,128)}, /*index=5*/f32[8,256,256]{2,1,0:T(8,128)}, s32[]{:T(128)}) while((s32[]{:T(128)}, f32[16,256]{1,0:T(8,128)S(1)}, f32[8,16,256]{2,1,0:T(8,128)}, f32[8,16,256]{2,1,0:T(8,128)S(1)}, ...), condition=%wide.region_25.26_spmd, body=%wide.region_24.25_spmd.sunk | while | flops 25169920 | bytes 624717 | solution.py:42
  262.5 20.4 %while.295 = (s32[]{:T(128)}, f32[16,256]{1,0:T(8,128)S(1)}, f32[8,16,256]{2,1,0:T(8,128)S(1)}, f32[8,256,256]{2,1,0:T(8,128)}, f32[8,256,256]{2,1,0:T(8,128)}, /*index=5*/s32[]{:T(128)}) while((s32[]{:T(128)}, f32[16,256]{1,0:T(8,128)S(1)}, f32[8,16,256]{2,1,0:T(8,128)S(1)}, f32[8,256,256]{2,1,0:T(8,128)}, f32[8,256,256]{2,1,0:T(8,128)}, ...), condition=%wide.region_27.28_spmd, body=%wide.region_26.27_spmd.sunk | while | flops 25169920 | bytes 607813 | solution.py:42
  282.9 5.8 %all-gather.5 = f32[64,256]{1,0:T(8,128)S(1)} all-gather(f32[16,256]{1,0:T(8,128)S(1)} %get-tuple-element.864), channel_id=7, replica_groups=mesh['grp'=2,'lvl'=4,'col'=4] {'lvl'}, dimensions={0}, use_global_device_ids=true | all-gather | bytes 81920 | tf_op jit(solution)/shard_map/all_gather | solution.py:20
  290.4 25.3 %while.297 = (s32[]{:T(128)}, f32[16,256]{1,0:T(8,128)S(1)}, f32[8,16,256]{2,1,0:T(8,128)}, f32[8,16,256]{2,1,0:T(8,128)S(1)}, f32[8,256,256]{2,1,0:T(8,128)}, /*index=5*/f32[8,256,256]{2,1,0:T(8,128)}, s32[]{:T(128)}) while((s32[]{:T(128)}, f32[16,256]{1,0:T(8,128)S(1)}, f32[8,16,256]{2,1,0:T(8,128)}, f32[8,16,256]{2,1,0:T(8,128)S(1)}, ...), condition=%wide.region_31.32_spmd, body=%wide.region_30.31_spmd.sunk | while | flops 25169920 | bytes 624717 | solution.py:42
  320.9 20.4 %while.298 = (s32[]{:T(128)}, f32[16,256]{1,0:T(8,128)S(1)}, f32[8,16,256]{2,1,0:T(8,128)S(1)}, f32[8,256,256]{2,1,0:T(8,128)}, f32[8,256,256]{2,1,0:T(8,128)}, /*index=5*/s32[]{:T(128)}) while((s32[]{:T(128)}, f32[16,256]{1,0:T(8,128)S(1)}, f32[8,16,256]{2,1,0:T(8,128)S(1)}, f32[8,256,256]{2,1,0:T(8,128)}, f32[8,256,256]{2,1,0:T(8,128)}, ...), condition=%wide.region_33.34_spmd, body=%wide.region_32.33_spmd.sunk | while | flops 25169920 | bytes 607813 | solution.py:42
  341.4 5.8 %all-gather.6 = f32[64,256]{1,0:T(8,128)S(1)} all-gather(f32[16,256]{1,0:T(8,128)S(1)} %get-tuple-element.867), channel_id=8, replica_groups=mesh['grp'=2,'lvl'=4,'col'=4] {'lvl'}, dimensions={0}, use_global_device_ids=true | all-gather | bytes 81920 | tf_op jit(solution)/shard_map/all_gather | solution.py:20
  348.9 25.3 %while.300 = (s32[]{:T(128)}, f32[16,256]{1,0:T(8,128)S(1)}, f32[8,16,256]{2,1,0:T(8,128)}, f32[8,16,256]{2,1,0:T(8,128)S(1)}, f32[8,256,256]{2,1,0:T(8,128)}, /*index=5*/f32[8,256,256]{2,1,0:T(8,128)}, s32[]{:T(128)}) while((s32[]{:T(128)}, f32[16,256]{1,0:T(8,128)S(1)}, f32[8,16,256]{2,1,0:T(8,128)}, f32[8,16,256]{2,1,0:T(8,128)S(1)}, ...), condition=%wide.region_37.38_spmd, body=%wide.region_36.37_spmd.sunk | while | flops 25169920 | bytes 624717 | solution.py:42
  379.4 20.4 %while.301 = (s32[]{:T(128)}, f32[16,256]{1,0:T(8,128)S(1)}, f32[8,16,256]{2,1,0:T(8,128)S(1)}, f32[8,256,256]{2,1,0:T(8,128)}, f32[8,256,256]{2,1,0:T(8,128)}, /*index=5*/s32[]{:T(128)}) while((s32[]{:T(128)}, f32[16,256]{1,0:T(8,128)S(1)}, f32[8,16,256]{2,1,0:T(8,128)S(1)}, f32[8,256,256]{2,1,0:T(8,128)}, f32[8,256,256]{2,1,0:T(8,128)}, ...), condition=%wide.region_39.40_spmd, body=%wide.region_38.39_spmd.sunk | while | flops 25169920 | bytes 607813 | solution.py:42
  399.8 5.8 %all-gather.7 = f32[64,256]{1,0:T(8,128)S(1)} all-gather(f32[16,256]{1,0:T(8,128)S(1)} %get-tuple-element.870), channel_id=9, replica_groups=mesh['grp'=2,'lvl'=4,'col'=4] {'lvl'}, dimensions={0}, use_global_device_ids=true | all-gather | bytes 81920 | tf_op jit(solution)/shard_map/all_gather | solution.py:20
  407.4 25.3 %while.303 = (s32[]{:T(128)}, f32[16,256]{1,0:T(8,128)S(1)}, f32[8,16,256]{2,1,0:T(8,128)}, f32[8,16,256]{2,1,0:T(8,128)S(1)}, f32[8,256,256]{2,1,0:T(8,128)}, /*index=5*/f32[8,256,256]{2,1,0:T(8,128)}, s32[]{:T(128)}) while((s32[]{:T(128)}, f32[16,256]{1,0:T(8,128)S(1)}, f32[8,16,256]{2,1,0:T(8,128)}, f32[8,16,256]{2,1,0:T(8,128)S(1)}, ...), condition=%wide.region_43.44_spmd, body=%wide.region_42.43_spmd.sunk | while | flops 25169920 | bytes 624717 | solution.py:42
  437.9 20.4 %while.304 = (s32[]{:T(128)}, f32[16,256]{1,0:T(8,128)S(1)}, f32[8,16,256]{2,1,0:T(8,128)S(1)}, f32[8,256,256]{2,1,0:T(8,128)}, f32[8,256,256]{2,1,0:T(8,128)}, /*index=5*/s32[]{:T(128)}) while((s32[]{:T(128)}, f32[16,256]{1,0:T(8,128)S(1)}, f32[8,16,256]{2,1,0:T(8,128)S(1)}, f32[8,256,256]{2,1,0:T(8,128)}, f32[8,256,256]{2,1,0:T(8,128)}, ...), condition=%wide.region_45.46_spmd, body=%wide.region_44.45_spmd.sunk | while | flops 25169920 | bytes 607813 | solution.py:42
  458.3 5.8 %all-gather.8 = f32[64,256]{1,0:T(8,128)S(1)} all-gather(f32[16,256]{1,0:T(8,128)S(1)} %get-tuple-element.873), channel_id=10, replica_groups=mesh['grp'=2,'lvl'=4,'col'=4] {'lvl'}, dimensions={0}, use_global_device_ids=true | all-gather | bytes 81920 | tf_op jit(solution)/shard_map/all_gather | solution.py:20
  465.2 20.4 %while.306 = (s32[]{:T(128)}, f32[16,256]{1,0:T(8,128)S(1)}, f32[8,16,256]{2,1,0:T(8,128)S(1)}, f32[8,16,256]{2,1,0:T(8,128)S(1)}, f32[8,256,256]{2,1,0:T(8,128)}, /*index=5*/f32[8,256,256]{2,1,0:T(8,128)}, s32[]{:T(128)}) while((s32[]{:T(128)}, f32[16,256]{1,0:T(8,128)S(1)}, f32[8,16,256]{2,1,0:T(8,128)S(1)}, ...), condition=%wide.region_49.50_spmd, body=%wide.region_48.49_spmd.sunk | while | flops 25169920 | bytes 624717 | solution.py:42
  (397 shorter events, 420.0 us)
Async XLA Ops:
  6.5 25.1 %copy-start = (f32[8,256,256]{2,1,0:T(8,128)S(1)}, f32[8,256,256]{2,1,0:T(8,128)}, u32[]{:S(2)}) copy-start(f32[8,256,256]{2,1,0:T(8,128)} %param.56) | copy-start | bytes 6291460
  6.5 52.5 %all-gather.11.cloned.1.call-start = ((), (), s32[]{:S(2)}) async-start(), calls=%async_computation | async-start | bytes 1310720 | tf_op jit(solution)/shard_map/all_gather | solution.py:20
  6.5 25.1 %collective-permute-start = (f32[16,256]{1,0:T(8,128)S(1)}, f32[16,256]{1,0:T(8,128)S(1)}, u32[]{:S(2)}, u32[]{:S(2)}) collective-permute-start(f32[16,256]{1,0:T(8,128)S(1)} %broadcast.8), channel_id=1, source_target_pairs={{4,0},{8,4},{12,8},{5,1},{9,5},{13,9},{6,2},{10,6},{14,10},{7,3},{... | collective-permute-start | bytes 49160 | tf_op jit(solution)/shard_map/ppermute | solution.py:15
  9.3 22.4 %copy-start.3 = (f32[8,16,256]{2,1,0:T(8,128)S(1)}, f32[8,16,256]{2,1,0:T(8,128)}, u32[]{:S(2)}) copy-start(f32[8,16,256]{2,1,0:T(8,128)} %param.57) | copy-start | bytes 393220
  30.9 0.7 copy-start.2
  83.5 2.1 collective-permute-start.1
  85.6 27.7 %copy-start.1 = (f32[4,256,256]{2,1,0:T(8,128)S(1)}, f32[4,256,256]{2,1,0:T(8,128)}, u32[]{:S(2)}) copy-start(f32[4,256,256]{2,1,0:T(8,128)} %get-tuple-element.2566) | copy-start | bytes 3145732
  141.0 2.6 collective-permute-start.2
  199.4 2.6 collective-permute-start.3
  258.0 2.6 collective-permute-start.4
  316.5 2.6 collective-permute-start.5
  374.9 2.6 collective-permute-start.6
  433.4 2.6 collective-permute-start.7
  485.6 0.7 copy-start.4
Sparse Core Ops, SparseCore 0:
  31.7 16.8 all-gather.10
where the time goes:
time: 503 us; the launch traced here: 493 us
  matrix products  394 us (78%)
  blocking collectives  45.4 us (9%)
  local copies, waits for them, and re-layouts  16 us (3%)
  starting transfers between devices  14.3 us (3%)
  between operations  13.8 us (3%)
  loops' own time  8.79 us (2%)
    dot_general x280, matrix products, apply_right(): return jnp.einsum('km,pm->kp', vector, matrix, precision=PRECISE)  358 us
    all_gather x8, blocking collectives, entering_2(): gathered = jax.tree.map(lambda a: lax.all_gather(a, axis), part)  45.4 us
    dot_general x8, matrix products, local(): jnp.einsum('lkm,lpm->lkp', beyond, up_block, precision=PRECISE)  14.7 us
    ppermute x8, starting transfers between devices, from_behind(): lax.ppermute(value, axis, [(source, source + steps) for source in range(f...  14.3 us
    dot_general x8, matrix products, compose(): jnp.matmul(down_here, product, precision=PRECISE)  10.7 us
    dot_general x8, matrix products, compose(): jnp.matmul(inv_here, jnp.matmul(down_here, product, precision=PRECISE), p...  10.7 us
  transfers between devices with their start and end apart: 9, of which 1 were waited for; matrix products, arithmetic and copies ran while one was open for 10% of the time, Pallas kernels for 0%

commit v1 on v0

v1 whole, which is shorter than its diff:
```python
import functools

import jax
import jax.numpy as jnp
from jax import lax
from jax.experimental import pallas as pl
from jax.experimental.pallas import tpu as pltpu
from jax.sharding import PartitionSpec as P

SWEEPS = 8
MESH = pl.DeviceIdType.MESH


def split(value):
    high = value.astype(jnp.bfloat16)
    low = (value - high.astype(jnp.float32)).astype(jnp.bfloat16)
    return high, low


def dot(left, right):
    return jnp.dot(left, right, preferred_element_type=jnp.float32)


def apply_split(vector, high, low):
    rows = vector.shape[0]
    rounded = vector.astype(jnp.bfloat16).astype(jnp.float32)
    stacked = jnp.concatenate([rounded, vector - rounded], axis=0).astype(jnp.bfloat16)
    both = dot(stacked, high)
    return both[:rows] + both[rows:] + dot(rounded.astype(jnp.bfloat16), low)


def kernel(
    count, inv_hbm, down_hbm, up_hbm, reward_ref, out_ref,
    inv, down, up, a_high, a_low, b_high, b_low, base, from_below, from_above, top, bottom,
    load_sem, below_recv, above_recv, top_send, bottom_send,
):
    levels, phases = inv_hbm.shape[0], inv_hbm.shape[1]
    place = lax.axis_index("lvl")
    first, last = place == 0, place == count - 1

    def loads(level):
        return [
            pltpu.make_async_copy(source.at[level], target.at[level], load_sem.at[kind, level])
            for kind, (source, target) in enumerate(
                ((inv_hbm, inv), (down_hbm, down), (up_hbm, up))
            )
        ]

    for level in range(levels):
        for copy in loads(level):
            copy.start()

    barrier = pltpu.get_barrier_semaphore()

    @pl.when(place > 0)
    def _():
        pl.semaphore_signal(barrier, inc=1, device_id={"lvl": place - 1}, device_id_type=MESH)

    @pl.when(place < count - 1)
    def _():
        pl.semaphore_signal(barrier, inc=1, device_id={"lvl": place + 1}, device_id_type=MESH)

    out_ref[...] = jnp.zeros_like(out_ref)

    @pl.when(first)
    def _():
        from_below[...] = jnp.zeros_like(from_below)

    @pl.when(last)
    def _():
        from_above[...] = jnp.zeros_like(from_above)

    @pl.when(place < count - 1)
    def _():
        from_above[0] = jnp.zeros_like(from_above[0])

    for level in range(levels):
        for copy in loads(level):
            copy.wait()
        inv_t_high, inv_t_low = split(inv[level].T)
        base[level] = apply_split(reward_ref[level], inv_t_high, inv_t_low)
        for block, high_ref, low_ref in ((down, a_high, a_low), (up, b_high, b_low)):
            block_high, block_low = split(block[level].T)
            product = dot(block_high, inv_t_high) + (
                dot(block_high, inv_t_low) + dot(block_low, inv_t_high)
            )
            high_ref[level], low_ref[level] = split(product)

    pl.semaphore_wait(barrier, jnp.minimum(place, 1) + jnp.minimum(count - 1 - place, 1))

    def going_up(sweep):
        return pltpu.make_async_remote_copy(
            src_ref=top.at[sweep], dst_ref=from_below.at[sweep],
            send_sem=top_send.at[sweep], recv_sem=below_recv.at[sweep],
            device_id={"lvl": place + 1}, device_id_type=MESH,
        )

    def going_down(sweep):
        return pltpu.make_async_remote_copy(
            src_ref=bottom.at[sweep], dst_ref=from_above.at[sweep + 1],
            send_sem=bottom_send.at[sweep], recv_sem=above_recv.at[sweep],
            device_id={"lvl": place - 1}, device_id_type=MESH,
        )

    def one_sweep(sweep, _):
        terms = [
            base[level] + apply_split(out_ref[level + 1], b_high[level], b_low[level])
            for level in range(levels - 1)
        ]

        @pl.when(place > 0)
        def _():
            going_up(sweep).wait_recv()

        carried = terms[0] + apply_split(from_below[sweep], a_high[0], a_low[0])
        out_ref[0] = carried

        @pl.when((place > 0) & (sweep < SWEEPS - 1))
        def _():
            bottom[sweep] = carried
            going_down(sweep).start()

        for level in range(1, levels - 1):
            carried = terms[level] + apply_split(carried, a_high[level], a_low[level])
            out_ref[level] = carried
        end = levels - 1
        partial = base[end] + apply_split(carried, a_high[end], a_low[end])

        @pl.when((place < count - 1) & (sweep > 0))
        def _():
            going_down(sweep - 1).wait_recv()

        carried = partial + apply_split(from_above[sweep], b_high[end], b_low[end])
        out_ref[end] = carried

        @pl.when(place < count - 1)
        def _():
            top[sweep] = carried
            going_up(sweep).start()

        return 0

    lax.fori_loop(0, SWEEPS, one_sweep, 0)

    for sweep in range(SWEEPS):
        @pl.when(place < count - 1)
        def _():
            going_up(sweep).wait_send()

        if sweep < SWEEPS - 1:
            @pl.when(place > 0)
            def _():
                going_down(sweep).wait_send()


def solution(mesh):
    count = mesh.shape["lvl"]

    def local(inverse_diag, down_block, up_block, reward):
        levels, rows, phases = reward.shape
        whole = (levels, phases, phases)
        wide = pltpu.VMEM(whole, jnp.float32)
        narrow = pltpu.VMEM(whole, jnp.bfloat16)
        edge = pltpu.VMEM((SWEEPS, rows, phases), jnp.float32)
        return pl.pallas_call(
            functools.partial(kernel, count),
            out_shape=jax.ShapeDtypeStruct(reward.shape, jnp.float32),
            in_specs=[pl.BlockSpec(memory_space=pl.ANY)] * 3
            + [pl.BlockSpec(memory_space=pltpu.VMEM)],
            out_specs=pl.BlockSpec(memory_space=pltpu.VMEM),
            scratch_shapes=[wide] * 3 + [narrow] * 4
            + [pltpu.VMEM(reward.shape, jnp.float32)] + [edge] * 4
            + [pltpu.SemaphoreType.DMA((3, levels))] + [pltpu.SemaphoreType.DMA((SWEEPS,))] * 4,
            compiler_params=pltpu.CompilerParams(
                collective_id=0, has_side_effects=True, vmem_limit_bytes=40 << 20
            ),
            name="sweeps",
        )(inverse_diag, down_block, up_block, reward)

    matrices = P(("grp", "lvl"), None, None)
    columns = P(("grp", "lvl"), "col", None)
    return jax.shard_map(
        local, mesh=mesh, in_specs=(matrices, matrices, matrices, columns),
        out_specs=columns, check_vma=False,
    )
```

time: 503 us -> 56.3 us (0.11); the launches traced: 493 us -> 56.1 us
  matrix products: 394 us -> 0 us
  Pallas kernels: 0 us -> 49.8 us
  blocking collectives: 45.4 us -> 0 us
  starting transfers between devices: 14.3 us -> 0 us
  between operations: 13.8 us -> 0.01 us
  local copies, waits for them, and re-layouts: 16 us -> 6.33 us
  loops' own time: 8.79 us -> 0 us
    dot_general x304 -> x0, matrix products: 394 us -> none  [the longest x280 358 us: apply_right(): return jnp.einsum('km,pm->kp', vector, matrix, precision=PRECISE)]
    pallas_call x0 -> x1, Pallas kernels: none -> 49.8 us  [local(): pl.pallas_call(functools.partial(kernel, count), out_shape=jax.ShapeDtype...]
    all_gather x8 -> x0, blocking collectives: 45.4 us -> none  [entering_2(): gathered = jax.tree.map(lambda a: lax.all_gather(a, axis), part)]
    ppermute x8 -> x0, starting transfers between devices: 14.3 us -> none  [from_behind(): lax.ppermute(value, axis, [(source, source + steps) for source in range(f...]
    another operation x25 -> x0, loops' own time: 8.79 us -> none  [the longest x16 7.71 us: local_sweep(): lax.scan(level_step, entering, (inverse_diag, down_block, base_terms))]
    slice x7 -> x0, local copies, waits for them, and re-layouts: 5.47 us -> none  [local(): beyond = jnp.concatenate([estimate[1:], rim_values[None]], axis=0)]
  transfers between devices with their start and end apart: 9 -> 0, of which waited for: 1 -> 0; matrix products, arithmetic and copies ran while one was open for 10% -> 0% of each run, Pallas kernels for 0% -> 0%
where the time goes in v1:
time: 56.3 us; the launch traced here: 56.1 us
  Pallas kernels  49.8 us (88%)
  local copies, waits for them, and re-layouts  6.33 us (11%)
    pallas_call x1, Pallas kernels, local(): pl.pallas_call(functools.partial(kernel, count), out_shape=jax.ShapeDtype...  49.8 us
    unnamed x9, local copies, waits for them, and re-layouts  6.33 us

profile of v1, /device:TPU:11, one launch (start us, length us, event | category | flops | bytes accessed | tf_op | source)
XLA Modules:
  0.0 56.1 jit_solution(8012709659763316664)
XLA Ops:
  0.0 0.0 copy-start
  0.0 1.6 %copy-done = f32[8,256,256]{2,1,0:T(8,128)S(1)} copy-done((f32[8,256,256]{2,1,0:T(8,128)S(1)}, f32[8,256,256]{2,1,0:T(8,128)}, u32[]{:S(2)}) %copy-start) | copy-done | bytes 2097176
  1.6 0.0 copy-start.1
  1.6 1.6 %copy-done.1 = f32[8,256,256]{2,1,0:T(8,128)S(1)} copy-done((f32[8,256,256]{2,1,0:T(8,128)S(1)}, f32[8,256,256]{2,1,0:T(8,128)}, u32[]{:S(2)}) %copy-start.1) | copy-done | bytes 2097176
  3.2 0.0 copy-start.2
  3.2 1.6 %copy-done.2 = f32[8,256,256]{2,1,0:T(8,128)S(1)} copy-done((f32[8,256,256]{2,1,0:T(8,128)S(1)}, f32[8,256,256]{2,1,0:T(8,128)}, u32[]{:S(2)}) %copy-start.2) | copy-done | bytes 2097176
  4.8 0.0 copy-start.3
  4.8 0.9 %copy-done.3 = f32[8,16,256]{2,1,0:T(8,128)S(1)} copy-done((f32[8,16,256]{2,1,0:T(8,128)S(1)}, f32[8,16,256]{2,1,0:T(8,128)}, u32[]{:S(2)}) %copy-start.3) | copy-done | bytes 131096
  5.7 49.8 %sweeps.1 = f32[8,16,256]{2,1,0:T(8,128)S(1)} custom-call(f32[8,256,256]{2,1,0:T(8,128)S(1)} %copy-done, f32[8,256,256]{2,1,0:T(8,128)S(1)} %copy-done.1, f32[8,256,256]{2,1,0:T(8,128)S(1)} %copy-done.2, f32[8,16,256]{2,1,0:T(8,128)S(1)} %copy-done.3), custom_call_target="tpu_custom_call" | custom-call | tf_op jit(solution)/shard_map/sweeps/pallas_call | solution.py:165
  55.4 0.7 %copy.6 = f32[8,16,256]{2,1,0:T(8,128)} copy(f32[8,16,256]{2,1,0:T(8,128)S(1)} %sweeps.1) | data formatting | bytes 262144
Async XLA Ops:
  0.0 1.6 %copy-start = (f32[8,256,256]{2,1,0:T(8,128)S(1)}, f32[8,256,256]{2,1,0:T(8,128)}, u32[]{:S(2)}) copy-start(f32[8,256,256]{2,1,0:T(8,128)} %inv_hbm.1) | copy-start | bytes 6291460
  1.6 1.6 %copy-start.1 = (f32[8,256,256]{2,1,0:T(8,128)S(1)}, f32[8,256,256]{2,1,0:T(8,128)}, u32[]{:S(2)}) copy-start(f32[8,256,256]{2,1,0:T(8,128)} %down_hbm.1) | copy-start | bytes 6291460
  3.2 1.6 %copy-start.2 = (f32[8,256,256]{2,1,0:T(8,128)S(1)}, f32[8,256,256]{2,1,0:T(8,128)}, u32[]{:S(2)}) copy-start(f32[8,256,256]{2,1,0:T(8,128)} %up_hbm.1) | copy-start | bytes 6291460
  4.8 0.9 %copy-start.3 = (f32[8,16,256]{2,1,0:T(8,128)S(1)}, f32[8,16,256]{2,1,0:T(8,128)}, u32[]{:S(2)}) copy-start(f32[8,16,256]{2,1,0:T(8,128)} %reward_ref.1) | copy-start | bytes 393220

commit v2 on v1

v2 whole, which is shorter than its diff:
```python
import functools

import jax
import jax.numpy as jnp
from jax import lax
from jax.experimental import pallas as pl
from jax.experimental.pallas import tpu as pltpu
from jax.sharding import PartitionSpec as P

SWEEPS = 8
MESH = pl.DeviceIdType.MESH


def split(value):
    high = value.astype(jnp.bfloat16)
    low = (value - high.astype(jnp.float32)).astype(jnp.bfloat16)
    return high, low


def dot(left, right):
    return jnp.dot(left, right, preferred_element_type=jnp.float32)


def apply_split(vector, high, low):
    rows = vector.shape[0]
    rounded = vector.astype(jnp.bfloat16).astype(jnp.float32)
    stacked = jnp.concatenate([rounded, vector - rounded], axis=0).astype(jnp.bfloat16)
    both = dot(stacked, high)
    return both[:rows] + both[rows:] + dot(rounded.astype(jnp.bfloat16), low)


def kernel(
    count, inv_hbm, down_hbm, up_hbm, reward_ref, out_ref,
    inv, down, up, a_high, a_low, b_high, b_low, base, from_below, from_above, top, bottom,
    edge_out, edge_in,
    load_sem, below_recv, above_recv, top_send, bottom_send, edge_send, edge_recv,
):
    levels = inv_hbm.shape[0]
    place = lax.axis_index("lvl")
    has_below, has_above = place > 0, place < count - 1
    at = dict(device_id_type=MESH)
    end = levels - 1

    def loads(level):
        return [
            pltpu.make_async_copy(source.at[level], target.at[level], load_sem.at[kind, level])
            for kind, (source, target) in enumerate(
                ((inv_hbm, inv), (down_hbm, down), (up_hbm, up))
            )
        ]

    for level in range(levels):
        for copy in loads(level):
            copy.start()

    barrier = pltpu.get_barrier_semaphore()

    @pl.when(has_below)
    def _():
        pl.semaphore_signal(barrier, inc=1, device_id={"lvl": place - 1}, **at)

    @pl.when(has_above)
    def _():
        pl.semaphore_signal(barrier, inc=1, device_id={"lvl": place + 1}, **at)

    out_ref[...] = jnp.zeros_like(out_ref)
    from_above[0:2] = jnp.zeros_like(from_above[0:2])

    @pl.when(place == 0)
    def _():
        from_below[...] = jnp.zeros_like(from_below)

    @pl.when(place == count - 1)
    def _():
        from_above[...] = jnp.zeros_like(from_above)
        edge_in[...] = jnp.zeros_like(edge_in)
        base[levels] = jnp.zeros_like(base[levels])

    def edge_copies():
        below = {"lvl": place - 1}
        pairs = (
            (base.at[0], base.at[levels]),
            (edge_out.at[0], edge_in.at[0]),
            (edge_out.at[1], edge_in.at[1]),
        )
        return [
            pltpu.make_async_remote_copy(
                src_ref=source, dst_ref=target, send_sem=edge_send.at[n], recv_sem=edge_recv.at[n],
                device_id=below, **at,
            )
            for n, (source, target) in enumerate(pairs)
        ]

    for level in range(levels):
        for copy in loads(level):
            copy.wait()
        inv_t_high, inv_t_low = split(inv[level].T)
        base[level] = apply_split(reward_ref[level], inv_t_high, inv_t_low)
        for kind, (block, high_ref, low_ref) in enumerate(
            ((down, a_high, a_low), (up, b_high, b_low))
        ):
            block_high, block_low = split(block[level].T)
            product = dot(block_high, inv_t_high) + (
                dot(block_high, inv_t_low) + dot(block_low, inv_t_high)
            )
            high_ref[level], low_ref[level] = split(product)
            if level == 0:
                edge_out[kind] = product
        if level == 0:
            pl.semaphore_wait(
                barrier, jnp.minimum(place, 1) + jnp.minimum(count - 1 - place, 1)
            )

            @pl.when(has_below)
            def _():
                for copy in edge_copies():
                    copy.start()

    def going_up(sweep):
        return pltpu.make_async_remote_copy(
            src_ref=top.at[sweep], dst_ref=from_below.at[sweep],
            send_sem=top_send.at[sweep], recv_sem=below_recv.at[sweep],
            device_id={"lvl": place + 1}, **at,
        )

    def going_down(sweep):
        return pltpu.make_async_remote_copy(
            src_ref=bottom.at[sweep], dst_ref=from_above.at[sweep + 2],
            send_sem=bottom_send.at[sweep], recv_sem=above_recv.at[sweep],
            device_id={"lvl": place - 1}, **at,
        )

    def await_below(sweep):
        @pl.when(has_below)
        def _():
            going_up(sweep).wait_recv()

        return from_below[sweep]

    def await_above(turn, sweep):
        @pl.when(has_above & (turn > 0))
        def _():
            going_down(sweep - 2).wait_recv()

        return from_above[sweep]

    def send_up(sweep, value):
        @pl.when(has_above)
        def _():
            top[sweep] = value
            going_up(sweep).start()

    def send_down(turn, sweep, value):
        @pl.when(has_below & (turn < SWEEPS // 2 - 1))
        def _():
            bottom[sweep] = value
            going_down(sweep).start()

    def times_a(value, level):
        return apply_split(value, a_high[level], a_low[level])

    def times_b(value, level):
        return apply_split(value, b_high[level], b_low[level])

    def two_sweeps(turn, _):
        even, odd = 2 * turn, 2 * turn + 1
        terms = [base[n] + times_b(out_ref[n + 1], n) for n in range(end)]
        old_end = out_ref[end]
        x, y = [None] * (levels + 1), [None] * levels

        x[0] = terms[0] + times_a(await_below(even), 0)
        x[1] = terms[1] + times_a(x[0], 1)
        send_down(turn, even, x[1])
        entering = await_below(odd)
        for step in range(2, end):
            low = step - 2
            x[step] = terms[step] + times_a(x[step - 1], step)
            y[low] = (base[low] + times_b(x[low + 1], low)) + times_a(
                entering if low == 0 else y[low - 1], low
            )
            if low == 1:
                send_down(turn, odd, y[1])

        @pl.when(turn == 0)
        def _():
            @pl.when(has_above)
            def _():
                for copy in edge_copies():
                    copy.wait_recv()

            a_high[levels], a_low[levels] = split(edge_in[0])
            b_high[levels], b_low[levels] = split(edge_in[1])

        after = base[levels] + times_a(old_end, levels) + times_b(await_above(turn, even), levels)
        after = jnp.where(turn > 0, after, jnp.zeros_like(after))
        x[end] = (base[end] + times_a(x[end - 1], end)) + times_b(after, end)
        send_up(even, x[end])
        low = end - 2
        y[low] = (base[low] + times_b(x[low + 1], low)) + times_a(y[low - 1], low)
        beyond = base[levels] + times_b(await_above(turn, odd), levels)
        x[levels] = beyond + times_a(x[end], levels)
        low = end - 1
        y[low] = (base[low] + times_b(x[end], low)) + times_a(y[low - 1], low)
        y[end] = (base[end] + times_a(y[end - 1], end)) + times_b(x[levels], end)
        send_up(odd, y[end])
        for n in range(levels):
            out_ref[n] = y[n]
        return 0

    lax.fori_loop(0, SWEEPS // 2, two_sweeps, 0)

    @pl.when(has_above)
    def _():
        for sweep in range(SWEEPS):
            going_up(sweep).wait_send()

    @pl.when(has_below)
    def _():
        for sweep in range(SWEEPS - 2):
            going_down(sweep).wait_send()
        for copy in edge_copies():
            copy.wait_send()


def solution(mesh):
    count = mesh.shape["lvl"]

    def local(inverse_diag, down_block, up_block, reward):
        levels, rows, phases = reward.shape
        whole = (levels, phases, phases)
        wide = pltpu.VMEM(whole, jnp.float32)
        narrow = pltpu.VMEM((levels + 1, phases, phases), jnp.bfloat16)
        edge = pltpu.VMEM((SWEEPS, rows, phases), jnp.float32)
        return pl.pallas_call(
            functools.partial(kernel, count),
            out_shape=jax.ShapeDtypeStruct(reward.shape, jnp.float32),
            in_specs=[pl.BlockSpec(memory_space=pl.ANY)] * 3
            + [pl.BlockSpec(memory_space=pltpu.VMEM)],
            out_specs=pl.BlockSpec(memory_space=pltpu.VMEM),
            scratch_shapes=[wide] * 3 + [narrow] * 4
            + [pltpu.VMEM((levels + 1, rows, phases), jnp.float32)] + [edge] * 4
            + [pltpu.VMEM((2, phases, phases), jnp.float32)] * 2
            + [pltpu.SemaphoreType.DMA((3, levels))] + [pltpu.SemaphoreType.DMA((SWEEPS,))] * 4
            + [pltpu.SemaphoreType.DMA((3,))] * 2,
            compiler_params=pltpu.CompilerParams(
                collective_id=0, has_side_effects=True, vmem_limit_bytes=62 << 20
            ),
            name="sweeps",
        )(inverse_diag, down_block, up_block, reward)

    matrices = P(("grp", "lvl"), None, None)
    columns = P(("grp", "lvl"), "col", None)
    return jax.shard_map(
        local, mesh=mesh, in_specs=(matrices, matrices, matrices, columns),
        out_specs=columns, check_vma=False,
    )
```

time: 56.3 us -> 39.2 us (0.70)
  Pallas kernels: 49.8 us -> 37.5 us
  local copies, waits for them, and re-layouts: 6.33 us -> 1.57 us
    pallas_call x1, Pallas kernels: 49.8 us -> 37.5 us  [local(): pl.pallas_call(functools.partial(kernel, count), out_shape=jax.ShapeDtype...]
    unnamed x9 -> x1, local copies, waits for them, and re-layouts: 6.33 us -> 1.57 us
where the time goes in v2:
time: 39.2 us; the launch traced here: 39 us
  Pallas kernels  37.5 us (96%)
  local copies, waits for them, and re-layouts  1.57 us (4%)
    pallas_call x1, Pallas kernels, local(): pl.pallas_call(functools.partial(kernel, count), out_shape=jax.ShapeDtype...  37.5 us
    unnamed x1, local copies, waits for them, and re-layouts  1.57 us

profile of v2, /device:TPU:11, one launch (start us, length us, event | category | flops | bytes accessed | tf_op | source)
XLA Modules:
  0.0 39.0 jit_solution(13722725394574990660)
XLA Ops:
  0.0 37.5 %sweeps.1 = f32[8,16,256]{2,1,0:T(8,128)} custom-call(f32[8,256,256]{2,1,0:T(8,128)} %inv_hbm.1, f32[8,256,256]{2,1,0:T(8,128)} %down_hbm.1, f32[8,256,256]{2,1,0:T(8,128)} %up_hbm.1, f32[8,16,256]{2,1,0:T(8,128)} %reward_ref.1), custom_call_target="tpu_custom_call" | custom-call | tf_op jit(solution)/shard_map/sweeps/pallas_call | solution.py:234
  37.5 1.6 %copy.6 = f32[8,16,256]{2,1,0:T(8,128)} copy(f32[8,16,256]{2,1,0:T(8,128)} %sweeps.1) | data formatting | bytes 262144

commit v3 on v2

--- a/solution.py
+++ b/solution.py
@@ -30,10 +30,10 @@
 
 
 def kernel(
-    count, inv_hbm, down_hbm, up_hbm, reward_ref, out_ref,
-    inv, down, up, a_high, a_low, b_high, b_low, base, from_below, from_above, top, bottom,
+    count, inv_hbm, down_hbm, up_hbm, reward_hbm, out_ref,
+    reward_ref, inv, down, up, a_high, a_low, b_high, b_low, base, from_below, from_above, top, bottom,
     edge_out, edge_in,
-    load_sem, below_recv, above_recv, top_send, bottom_send, edge_send, edge_recv,
+    reward_sem, load_sem, below_recv, above_recv, top_send, bottom_send, edge_send, edge_recv,
 ):
     levels = inv_hbm.shape[0]
     place = lax.axis_index("lvl")
@@ -49,9 +49,12 @@
             )
         ]
 
+    reward_load = pltpu.make_async_copy(reward_hbm, reward_ref, reward_sem)
     for level in range(levels):
         for copy in loads(level):
             copy.start()
+        if level == 0:
+            reward_load.start()
 
     barrier = pltpu.get_barrier_semaphore()
 
@@ -91,9 +94,13 @@
             for n, (source, target) in enumerate(pairs)
         ]
 
+    half = levels // 2
+    reward_load.wait()
     for level in range(levels):
-        for copy in loads(level):
-            copy.wait()
+        if level % half == 0:
+            for member in range(level, level + half):
+                for copy in loads(member):
+                    copy.wait()
         inv_t_high, inv_t_low = split(inv[level].T)
         base[level] = apply_split(reward_ref[level], inv_t_high, inv_t_low)
         for kind, (block, high_ref, low_ref) in enumerate(
@@ -106,7 +113,7 @@
             high_ref[level], low_ref[level] = split(product)
             if level == 0:
                 edge_out[kind] = product
-        if level == 0:
+        if level == half - 1:
             pl.semaphore_wait(
                 barrier, jnp.minimum(place, 1) + jnp.minimum(count - 1 - place, 1)
             )
@@ -234,13 +241,13 @@
         return pl.pallas_call(
             functools.partial(kernel, count),
             out_shape=jax.ShapeDtypeStruct(reward.shape, jnp.float32),
-            in_specs=[pl.BlockSpec(memory_space=pl.ANY)] * 3
-            + [pl.BlockSpec(memory_space=pltpu.VMEM)],
+            in_specs=[pl.BlockSpec(memory_space=pl.ANY)] * 4,
             out_specs=pl.BlockSpec(memory_space=pltpu.VMEM),
-            scratch_shapes=[wide] * 3 + [narrow] * 4
+            scratch_shapes=[pltpu.VMEM(reward.shape, jnp.float32)] + [wide] * 3 + [narrow] * 4
             + [pltpu.VMEM((levels + 1, rows, phases), jnp.float32)] + [edge] * 4
             + [pltpu.VMEM((2, phases, phases), jnp.float32)] * 2
-            + [pltpu.SemaphoreType.DMA((3, levels))] + [pltpu.SemaphoreType.DMA((SWEEPS,))] * 4
+            + [pltpu.SemaphoreType.DMA, pltpu.SemaphoreType.DMA((3, levels))]
+            + [pltpu.SemaphoreType.DMA((SWEEPS,))] * 4
             + [pltpu.SemaphoreType.DMA((3,))] * 2,
             compiler_params=pltpu.CompilerParams(
                 collective_id=0, has_side_effects=True, vmem_limit_bytes=62 << 20

time: 39.2 us -> 40.4 us (1.031)
  Pallas kernels: 37.5 us -> 38.7 us
    pallas_call x1, Pallas kernels: 37.5 us -> 38.7 us  [local(): pl.pallas_call(functools.partial(kernel, count), out_shape=jax.ShapeDtype...]
where the time goes in v3:
time: 40.4 us; the launch traced here: 40.3 us
  Pallas kernels  38.7 us (96%)
  local copies, waits for them, and re-layouts  1.57 us (4%)
    pallas_call x1, Pallas kernels, local(): pl.pallas_call(functools.partial(kernel, count), out_shape=jax.ShapeDtype...  38.7 us
    unnamed x1, local copies, waits for them, and re-layouts  1.57 us

profile of v3, /device:TPU:11, one launch (start us, length us, event | category | flops | bytes accessed | tf_op | source)
XLA Modules:
  0.0 40.3 jit_solution(8371684858632623481)
XLA Ops:
  0.0 38.7 %sweeps.1 = f32[8,16,256]{2,1,0:T(8,128)} custom-call(f32[8,256,256]{2,1,0:T(8,128)} %inv_hbm.1, f32[8,256,256]{2,1,0:T(8,128)} %down_hbm.1, f32[8,256,256]{2,1,0:T(8,128)} %up_hbm.1, f32[8,16,256]{2,1,0:T(8,128)} %reward_hbm.1), custom_call_target="tpu_custom_call" | custom-call | tf_op jit(solution)/shard_map/sweeps/pallas_call | solution.py:241
  38.7 1.6 %copy.6 = f32[8,16,256]{2,1,0:T(8,128)} copy(f32[8,16,256]{2,1,0:T(8,128)} %sweeps.1) | data formatting | bytes 262144

commit v4 on v3

--- a/solution.py
+++ b/solution.py
@@ -94,11 +94,11 @@
             for n, (source, target) in enumerate(pairs)
         ]
 
-    half = levels // 2
+    groups = {0: [0], 1: range(1, levels // 2), levels // 2: range(levels // 2, levels)}
     reward_load.wait()
     for level in range(levels):
-        if level % half == 0:
-            for member in range(level, level + half):
+        if level in groups:
+            for member in groups[level]:
                 for copy in loads(member):
                     copy.wait()
         inv_t_high, inv_t_low = split(inv[level].T)
@@ -113,7 +113,7 @@
             high_ref[level], low_ref[level] = split(product)
             if level == 0:
                 edge_out[kind] = product
-        if level == half - 1:
+        if level == 0:
             pl.semaphore_wait(
                 barrier, jnp.minimum(place, 1) + jnp.minimum(count - 1 - place, 1)
             )
@@ -192,10 +192,19 @@
         def _():
             @pl.when(has_above)
             def _():
-                for copy in edge_copies():
+                for copy in edge_copies()[:2]:
                     copy.wait_recv()
 
             a_high[levels], a_low[levels] = split(edge_in[0])
+            b_high[levels] = jnp.zeros_like(b_high[levels])
+            b_low[levels] = jnp.zeros_like(b_low[levels])
+
+        @pl.when(turn == 1)
+        def _():
+            @pl.when(has_above)
+            def _():
+                edge_copies()[2].wait_recv()
+
             b_high[levels], b_low[levels] = split(edge_in[1])
 
         after = base[levels] + times_a(old_end, levels) + times_b(await_above(turn, even), levels)

time: 40.4 us -> 38.3 us (0.948)
  Pallas kernels: 38.7 us -> 36.6 us
    pallas_call x1, Pallas kernels: 38.7 us -> 36.6 us  [local(): pl.pallas_call(functools.partial(kernel, count), out_shape=jax.ShapeDtype...]
where the time goes in v4:
time: 38.3 us; the launch traced here: 38.2 us
  Pallas kernels  36.6 us (96%)
  local copies, waits for them, and re-layouts  1.57 us (4%)
    pallas_call x1, Pallas kernels, local(): pl.pallas_call(functools.partial(kernel, count), out_shape=jax.ShapeDtype...  36.6 us
    unnamed x1, local copies, waits for them, and re-layouts  1.57 us

profile of v4, /device:TPU:11, one launch (start us, length us, event | category | flops | bytes accessed | tf_op | source)
XLA Modules:
  0.0 38.2 jit_solution(10078293812237197235)
XLA Ops:
  0.0 36.6 %sweeps.1 = f32[8,16,256]{2,1,0:T(8,128)} custom-call(f32[8,256,256]{2,1,0:T(8,128)} %inv_hbm.1, f32[8,256,256]{2,1,0:T(8,128)} %down_hbm.1, f32[8,256,256]{2,1,0:T(8,128)} %up_hbm.1, f32[8,16,256]{2,1,0:T(8,128)} %reward_hbm.1), custom_call_target="tpu_custom_call" | custom-call | tf_op jit(solution)/shard_map/sweeps/pallas_call | solution.py:250
  36.6 1.6 %copy.6 = f32[8,16,256]{2,1,0:T(8,128)} copy(f32[8,16,256]{2,1,0:T(8,128)} %sweeps.1) | data formatting | bytes 262144

commit v5 on v4

--- a/solution.py
+++ b/solution.py
@@ -113,15 +113,15 @@
             high_ref[level], low_ref[level] = split(product)
             if level == 0:
                 edge_out[kind] = product
-        if level == 0:
-            pl.semaphore_wait(
-                barrier, jnp.minimum(place, 1) + jnp.minimum(count - 1 - place, 1)
-            )
-
-            @pl.when(has_below)
-            def _():
-                for copy in edge_copies():
-                    copy.start()
+                if kind == 0:
+                    pl.semaphore_wait(
+                        barrier, jnp.minimum(place, 1) + jnp.minimum(count - 1 - place, 1)
+                    )
+
+                @pl.when(has_below)
+                def _():
+                    for copy in edge_copies()[:2] if kind == 0 else edge_copies()[2:]:
+                        copy.start()
 
     def going_up(sweep):
         return pltpu.make_async_remote_copy(

time: 38.3 us -> 38.7 us (1.010)
  no operation moved by 1% of the time
where the time goes in v5:
time: 38.7 us; the launch traced here: 38.5 us
  Pallas kernels  36.9 us (95%)
  local copies, waits for them, and re-layouts  1.57 us (4%)
    pallas_call x1, Pallas kernels, local(): pl.pallas_call(functools.partial(kernel, count), out_shape=jax.ShapeDtype...  36.9 us
    unnamed x1, local copies, waits for them, and re-layouts  1.57 us

profile of v5, /device:TPU:11, one launch (start us, length us, event | category | flops | bytes accessed | tf_op | source)
XLA Modules:
  0.0 38.5 jit_solution(417360403317433363)
XLA Ops:
  0.0 36.9 %sweeps.1 = f32[8,16,256]{2,1,0:T(8,128)} custom-call(f32[8,256,256]{2,1,0:T(8,128)} %inv_hbm.1, f32[8,256,256]{2,1,0:T(8,128)} %down_hbm.1, f32[8,256,256]{2,1,0:T(8,128)} %up_hbm.1, f32[8,16,256]{2,1,0:T(8,128)} %reward_hbm.1), custom_call_target="tpu_custom_call" | custom-call | tf_op jit(solution)/shard_map/sweeps/pallas_call | solution.py:250
  36.9 1.6 %copy.6 = f32[8,16,256]{2,1,0:T(8,128)} copy(f32[8,16,256]{2,1,0:T(8,128)} %sweeps.1) | data formatting | bytes 262144
